TPU v7x, 256 devices: a whole 4x4x8 slice. The times are simulated.
256 devices in a mesh: own: 64 (over z, x, core), grp: 4 (over y).
Axes of the slice: x: 4, y: 4, z: 8, core: 2. Of those that a mesh axis runs over, the one named last changes fastest.
Arguments:
- panel: float32 [64, 4, 768, 768], P('own', 'grp'), may hold values from -6 to 6
- diag_inverse: float32 [64, 768, 768], P('own', 'grp'), as said below
- ancestor: float32 [64, 4, 768, 768], P('own', 'grp'), may hold values from -6 to 6
- live_blocks: int32 [64], P('own'), may hold values from 1 to 4
- pair_first: int32 [64, 4, 7], P('own', 'grp'), may hold values from 0 to 3
- pair_second: int32 [64, 4, 7], P('own', 'grp'), may hold values from 0 to 3
- pair_offset: int32 [64, 4, 7], P('own', 'grp'), may hold values from 0 to 4
Outputs:
- solved: float32 [64, 4, 768, 768], P('own', 'grp')
- updated: float32 [64, 4, 768, 768], P('own', 'grp')
Inputs may be any that keep to these rules, and one draw needn't show every extreme that they name: diag_inverse[s] is upper triangular with a positive diagonal.
All inputs are finite; a program needn't handle non-finite values.
Results may differ from a plain program's by a relative error of at most 0.0001.
Values sent between devices are 32-bit elements; how exact they have to be, the bound alone decides.
A program may use at most 128 MiB of HBM per device.

v0:
```python
import jax
import jax.numpy as jnp
from jax import lax
from jax.sharding import PartitionSpec as P

REACH = 5


def joined_along(parts, dim):
    parts = jnp.moveaxis(parts, 0, dim)
    lengths = parts.shape
    return parts.reshape(*lengths[:dim], lengths[dim] * lengths[dim + 1], *lengths[dim + 2 :])


def copy_for_each(array, axis):
    copies = jnp.broadcast_to(array, (lax.axis_size(axis), *array.shape))
    return lax.all_to_all(copies, axis, split_axis=0, concat_axis=0, tiled=True)


def gather_directly(array, axis, dim):
    return joined_along(copy_for_each(array, axis), dim)


def passed_along(array, axis, by):
    size = lax.axis_size(axis)
    return lax.ppermute(array, axis, [(i, (i + by) % size) for i in range(size)])


def shards(panel, diag_inverse, ancestor, live_blocks, pair_first, pair_second, pair_offset):
    group_index = lax.axis_index("grp")
    factor = gather_directly(diag_inverse, "grp", 1)
    alive = (group_index < live_blocks[0]).astype(jnp.float32)
    solved = alive * jnp.dot(panel[0, 0], factor[0], precision=lax.Precision.HIGHEST)
    column = lax.all_gather(solved[None], "grp", axis=0, tiled=True)
    first = column[pair_first[0, 0]]
    second = column[pair_second[0, 0]]
    terms = jnp.einsum("pij,pkj->pik", first, second, precision=lax.Precision.HIGHEST)
    distances = jnp.arange(REACH, dtype=jnp.int32)
    weights = (pair_offset[0, 0][None, :] == distances[:, None]).astype(jnp.float32)
    outgoing = jnp.einsum("dp,pik->dik", weights, terms, precision=lax.Precision.HIGHEST)
    received = outgoing[0]
    for distance in range(1, REACH):
        received = received + passed_along(outgoing[distance], "own", distance)
    updated = ancestor[0, 0] - received
    return (solved[None, None], updated[None, None])


def solution(mesh):
    placed = (
        P("own", "grp", None, None),
        P("own", "grp", None),
        P("own", "grp", None, None),
        P("own"),
        P("own", "grp", None),
        P("own", "grp", None),
        P("own", "grp", None),
    )
    return jax.shard_map(
        shards,
        mesh=mesh,
        in_specs=placed,
        out_specs=(P("own", "grp", None, None), P("own", "grp", None, None)),
        check_vma=False,
    )
```

profile of v0, /device:TPU:33, one launch (start us, length us, event | category | flops | bytes accessed | tf_op | source)
XLA Modules:
  0.0 480.2 jit_solution(4008402591965512278)
XLA Ops:
  7.2 0.0 copy-start
  7.2 2.8 broadcast_in_dim.15
  10.0 4.5 all-to-all-start
  14.5 0.0 all-gather.3.cloned.1.call-start
  15.2 27.9 %all-to-all-done = f32[4,1,192,768]{3,2,1,0:T(8,128)} async-done(((f32[4,1,192,768]{3,2,1,0:T(8,128)}), f32[4,1,192,768]{3,2,1,0:T(8,128)}, u32[]{:S(2)}, u32[]{:S(2)}) %all-to-all-start) | async-done | bytes 2359328 | tf_op jit(solution)/shard_map/all_to_all | solution.py:17
  43.1 0.0 copy-done
  43.1 8.9 %fusion.10 = f32[768,768]{1,0:T(8,128)} fusion(f32[768,768]{1,0:T(8,128)} %bitcast.3, f32[1,1,768,768]{3,2,1,0:T(8,128)S(1)} %copy-done, f32[]{:T(128)S(6)} %convert_element_type.4), kind=kOutput, calls=%fused_computation.17 | convolution fusion | flops 5436407808 | bytes 7077892 | tf_op jit(solution)/shard_map/dot_general | solution.py:33
  52.0 0.0 all-gather.3.cloned.1.call-update
  52.0 0.6 copy-done.5
  52.7 0.0 copy-done.6
  52.7 95.5 %all-gather.3.cloned.1.call-done = f32[3072,768]{1,0:T(8,128)} async-done(((f32[768,768]{1,0:T(8,128)}), f32[3072,768]{1,0:T(8,128)}) %all-gather.3.cloned.1.call-update) | async-done | bytes 9437200 | tf_op jit(solution)/shard_map/all_gather | solution.py:34
  148.2 12.0 %gather_fusion.1 = f32[7,768,768]{2,1,0:T(8,128)} fusion(f32[4,768,768]{2,1,0:T(8,128)} %bitcast.56, s32[1024]{0:T(1024)S(1)} %pad_clamp_fusion), kind=kCustom, calls=%fused_computation.1 | custom fusion | bytes 33030172 | tf_op jit(solution)/shard_map/gather | solution.py:36
  160.2 11.8 %gather_fusion = f32[7,768,768]{2,1,0:T(8,128)} fusion(f32[4,768,768]{2,1,0:T(8,128)} %bitcast.57, s32[1024]{0:T(1024)S(1)} %pad_clamp_fusion.1), kind=kCustom, calls=%fused_computation | custom fusion | bytes 33030172 | tf_op jit(solution)/shard_map/gather | solution.py:35
  172.0 44.7 %fusion.19 = f32[7,768,768]{2,1,0:T(8,128)} fusion(f32[7,768,768]{2,1,0:T(8,128)} %gather_fusion, f32[7,768,768]{2,1,0:T(8,128)} %gather_fusion.1), kind=kOutput, calls=%fused_computation.28 | convolution fusion | flops 38050725888 | bytes 49545216 | tf_op jit(solution)/shard_map/pij,pkj->pik/dot_general | solution.py:37
  216.7 0.0 copy-done.4
  216.7 27.1 %fusion = f32[5,768,768]{2,0,1:T(8,128)} fusion(f32[7,768,768]{2,1,0:T(8,128)} %fusion.19, s32[7]{0:T(128)S(1)} %bitcast.64), kind=kOutput, calls=%fused_computation.2 | convolution fusion | flops 247726112 | bytes 28311580 | tf_op jit(solution)/shard_map/dp,pik->dik/dot_general | solution.py:40
  243.8 39.0 %fusion.18 = (f32[1,768,768]{2,0,1:T(1,128)}, f32[1,768,768]{2,0,1:T(1,128)S(1)}, f32[1,768,768]{2,0,1:T(1,128)S(1)}, f32[1,768,768]{2,0,1:T(1,128)S(1)}, f32[1,768,768]{2,0,1:T(1,128)S(1)}) fusion(f32[5,768,768]{2,0,1:T(8,128)} %fusion), kind=kLoop, calls=%fused_computation.27 | loop fusion | bytes 23592960 | tf_op jit(solution)/shard_map/slice | solution.py:41
  282.8 0.2 copy.39
  283.0 0.2 copy.40
  283.2 0.2 copy.41
  283.3 0.0 copy-start.2
  283.3 0.0 copy-start.3
  283.3 0.2 copy.38
  283.5 3.1 collective-permute-start.2
  286.6 1.3 collective-permute-start.3
  287.8 0.3 collective-permute-start
  288.1 0.9 collective-permute-start.1
  289.0 56.4 %collective-permute-done.2 = f32[768,768]{1,0:T(8,128)S(1)} collective-permute-done((f32[768,768]{1,0:T(8,128)S(1)}, f32[768,768]{1,0:T(8,128)S(1)}, u32[]{:S(2)}, u32[]{:S(2)}) %collective-permute-start.2) | collective-permute-done | bytes 2359328 | tf_op jit(solution)/shard_map/ppermute | solution.py:26
  345.5 44.3 %collective-permute-done.3 = f32[768,768]{1,0:T(8,128)S(1)} collective-permute-done((f32[768,768]{1,0:T(8,128)S(1)}, f32[768,768]{1,0:T(8,128)S(1)}, u32[]{:S(2)}, u32[]{:S(2)}) %collective-permute-start.3) | collective-permute-done | bytes 2359328 | tf_op jit(solution)/shard_map/ppermute | solution.py:26
  389.8 47.5 %collective-permute-done = f32[768,768]{1,0:T(8,128)S(1)} collective-permute-done((f32[768,768]{1,0:T(8,128)S(1)}, f32[768,768]{1,0:T(8,128)S(1)}, u32[]{:S(2)}, u32[]{:S(2)}) %collective-permute-start) | collective-permute-done | bytes 2359328 | tf_op jit(solution)/shard_map/ppermute | solution.py:26
  437.3 33.7 %collective-permute-done.1 = f32[768,768]{1,0:T(8,128)S(1)} collective-permute-done((f32[768,768]{1,0:T(8,128)S(1)}, f32[768,768]{1,0:T(8,128)S(1)}, u32[]{:S(2)}, u32[]{:S(2)}) %collective-permute-start.1) | collective-permute-done | bytes 2359328 | tf_op jit(solution)/shard_map/ppermute | solution.py:26
  471.0 2.3 fusion.7
  (11 shorter events, 0.0 us)
Async XLA Ops:
  7.2 35.9 %copy-start = (f32[1,1,768,768]{3,2,1,0:T(8,128)S(1)}, f32[1,1,768,768]{3,2,1,0:T(8,128)}, u32[]{:S(2)}) copy-start(f32[1,1,768,768]{3,2,1,0:T(8,128)} %param.7) | copy-start | bytes 7077892
  10.0 33.1 %all-to-all-start = ((f32[4,1,192,768]{3,2,1,0:T(8,128)}), f32[4,1,192,768]{3,2,1,0:T(8,128)}, u32[]{:S(2)}, u32[]{:S(2)}) async-start(f32[4,1,192,768]{3,2,1,0:T(8,128)} %broadcast_in_dim.15), calls=%async_computation | async-start | bytes 4718592 | tf_op jit(solution)/shard_map/all_to_all | solution.py:17
  14.5 133.7 %all-gather.3.cloned.1.call-start = ((), (), s32[]{:S(2)}) async-start(), calls=%async_computation.1 | async-start | bytes 11796480 | tf_op jit(solution)/shard_map/all_gather | solution.py:34
  52.0 0.7 copy-start.5
  52.0 0.7 copy-start.6
  172.0 44.7 %copy-start.4 = (s32[1,1,7]{2,1,0:T(1,128)S(1)}, s32[1,1,7]{2,1,0:T(1,128)}, u32[]{:S(2)}) copy-start(s32[1,1,7]{2,1,0:T(1,128)} %param.13) | copy-start | bytes 88
  283.3 187.7 %copy-start.2 = (f32[1,768,768]{2,0,1:T(1,128)S(1)}, f32[1,768,768]{2,0,1:T(1,128)}, u32[]{:S(2)}) copy-start(f32[1,768,768]{2,0,1:T(1,128)} %get-tuple-element.2) | copy-start | bytes 7077892
  283.3 187.7 %copy-start.3 = (f32[1,1,768,768]{3,2,1,0:T(8,128)S(1)}, f32[1,1,768,768]{3,2,1,0:T(8,128)}, u32[]{:S(2)}) copy-start(f32[1,1,768,768]{3,2,1,0:T(8,128)} %param.9) | copy-start | bytes 7077892
  283.5 62.0 %collective-permute-start.2 = (f32[768,768]{1,0:T(8,128)S(1)}, f32[768,768]{1,0:T(8,128)S(1)}, u32[]{:S(2)}, u32[]{:S(2)}) collective-permute-start(f32[768,768]{1,0:T(8,128)S(1)} %bitcast.62), channel_id=1, source_target_pairs={{0,12},{4,16},{8,20},{12,24},{16,28},{20,32},{24,36},{28,40},{32,4... | collective-permute-start | bytes 7077896 | tf_op jit(solution)/shard_map/ppermute | solution.py:26
  286.6 103.2 %collective-permute-start.3 = (f32[768,768]{1,0:T(8,128)S(1)}, f32[768,768]{1,0:T(8,128)S(1)}, u32[]{:S(2)}, u32[]{:S(2)}) collective-permute-start(f32[768,768]{1,0:T(8,128)S(1)} %bitcast.61), channel_id=1, source_target_pairs={{0,16},{4,20},{8,24},{12,28},{16,32},{20,36},{24,40},{28,44},{32,4... | collective-permute-start | bytes 7077896 | tf_op jit(solution)/shard_map/ppermute | solution.py:26
  287.8 149.5 %collective-permute-start = (f32[768,768]{1,0:T(8,128)S(1)}, f32[768,768]{1,0:T(8,128)S(1)}, u32[]{:S(2)}, u32[]{:S(2)}) collective-permute-start(f32[768,768]{1,0:T(8,128)S(1)} %bitcast.60), channel_id=1, source_target_pairs={{0,4},{4,8},{8,12},{12,16},{16,20},{20,24},{24,28},{28,32},{32,36}... | collective-permute-start | bytes 7077896 | tf_op jit(solution)/shard_map/ppermute | solution.py:26
  288.1 182.9 %collective-permute-start.1 = (f32[768,768]{1,0:T(8,128)S(1)}, f32[768,768]{1,0:T(8,128)S(1)}, u32[]{:S(2)}, u32[]{:S(2)}) collective-permute-start(f32[768,768]{1,0:T(8,128)S(1)} %bitcast.59), channel_id=1, source_target_pairs={{0,8},{4,12},{8,16},{12,20},{16,24},{20,28},{24,32},{28,36},{32,40... | collective-permute-start | bytes 7077896 | tf_op jit(solution)/shard_map/ppermute | solution.py:26
  471.0 2.3 copy-start.1
Sparse Core Ops, SparseCore 0:
  52.1 96.0 all-gather.2
where the time goes:
time: 480 us
  waiting for transfers between devices  305 us (64%)
  matrix products  80.8 us (17%)
  local copies, waits for them, and re-layouts  66.9 us (14%)
  between operations  14.8 us (3%)
  starting transfers between devices  10 us (2%)
    ppermute x4, waiting for transfers between devices, passed_along(): lax.ppermute(array, axis, [(i, (i + by) % size) for i in range(size)])  182 us
    all_gather x1, waiting for transfers between devices, shards(): column = lax.all_gather(solved[None], 'grp', axis=0, tiled=True)  95.5 us
    dot_general x1, matrix products, shards(): jnp.einsum('pij,pkj->pik', first, second, precision=lax.Precision.HIGHEST)  44.7 us
    slice x1, local copies, waits for them, and re-layouts, shards(): received = outgoing[0]  39 us
    all_to_all x1, waiting for transfers between devices, copy_for_each(): return lax.all_to_all(copies, axis, split_axis=0, concat_axis=0, tiled=True)  27.9 us
    dot_general x1, matrix products, shards(): jnp.einsum('dp,pik->dik', weights, terms, precision=lax.Precision.HIGHEST)  27.1 us
    gather x1, local copies, waits for them, and re-layouts, shards(): second = column[pair_second[0, 0]]  12 us
    gather x1, local copies, waits for them, and re-layouts, shards(): first = column[pair_first[0, 0]]  11.8 us
  transfers between devices with their start and end apart: 6, of which 6 were waited for; matrix products, arithmetic and copies ran while one was open for 0% of the time, Pallas kernels for 0%

commit v1 on v0

--- a/solution.py
+++ b/solution.py
@@ -31,7 +31,12 @@
     factor = gather_directly(diag_inverse, "grp", 1)
     alive = (group_index < live_blocks[0]).astype(jnp.float32)
     solved = alive * jnp.dot(panel[0, 0], factor[0], precision=lax.Precision.HIGHEST)
-    column = lax.all_gather(solved[None], "grp", axis=0, tiled=True)
+    ring = [solved[None]]
+    for hop in range(3):
+        ring.append(lax.ppermute(ring[-1], "grp", [(dev, (dev + 1) % 4) for dev in range(4)]))
+    column = jnp.roll(
+        jnp.concatenate(ring[::-1], axis=0), (lax.axis_index("grp") + 1) * ring[0].shape[0], axis=0
+    )
     first = column[pair_first[0, 0]]
     second = column[pair_second[0, 0]]
     terms = jnp.einsum("pij,pkj->pik", first, second, precision=lax.Precision.HIGHEST)

time: 480 us -> 566 us (1.18); the launches traced: 480 us -> 559 us
  waiting for transfers between devices: 305 us -> 362 us
  local copies, waits for them, and re-layouts: 66.9 us -> 96.9 us
  between operations: 14.8 us -> 1.66 us
    ppermute x0 -> x3, waiting for transfers between devices: none -> 154 us  [shards(): lax.ppermute(ring[-1], 'grp', [(dev, (dev + 1) % 4) for dev in range(4)])]
    all_gather x1 -> x0, waiting for transfers between devices: 95.5 us -> none  [shards(): column = lax.all_gather(solved[None], 'grp', axis=0, tiled=True)]
    unnamed x18 -> x33, local copies, waits for them, and re-layouts: 1.28 us -> 21.9 us
    dynamic_slice x0 -> x1, local copies, waits for them, and re-layouts: none -> 7.86 us  [shards(): jnp.roll(jnp.concatenate(ring[::-1], axis=0), (lax.axis_index('grp') + 1)...]
  transfers between devices with their start and end apart: 6 -> 8, of which waited for: 6 -> 8; matrix products, arithmetic and copies ran while one was open for 0% -> 0% of each run, Pallas kernels for 0% -> 0%
where the time goes in v1:
time: 566 us; the launch traced here: 559 us
  waiting for transfers between devices  362 us (64%)
  local copies, waits for them, and re-layouts  96.9 us (17%)
  matrix products  81.1 us (14%)
  starting transfers between devices  14.9 us (3%)
    ppermute x4, waiting for transfers between devices, passed_along(): lax.ppermute(array, axis, [(i, (i + by) % size) for i in range(size)])  180 us
    ppermute x3, waiting for transfers between devices, shards(): lax.ppermute(ring[-1], 'grp', [(dev, (dev + 1) % 4) for dev in range(4)])  154 us
    dot_general x1, matrix products, shards(): jnp.einsum('pij,pkj->pik', first, second, precision=lax.Precision.HIGHEST)  44.7 us
    slice x1, local copies, waits for them, and re-layouts, shards(): received = outgoing[0]  39.2 us
    all_to_all x1, waiting for transfers between devices, copy_for_each(): return lax.all_to_all(copies, axis, split_axis=0, concat_axis=0, tiled=True)  27.9 us
    dot_general x1, matrix products, shards(): jnp.einsum('dp,pik->dik', weights, terms, precision=lax.Precision.HIGHEST)  27.3 us
    unnamed x33, local copies, waits for them, and re-layouts  21.9 us
    gather x1, local copies, waits for them, and re-layouts, shards(): second = column[pair_second[0, 0]]  11.8 us
  transfers between devices with their start and end apart: 8, of which 8 were waited for; matrix products, arithmetic and copies ran while one was open for 0% of the time, Pallas kernels for 0%

profile of v1, /device:TPU:33, one launch (start us, length us, event | category | flops | bytes accessed | tf_op | source)
XLA Modules:
  0.0 559.0 jit_solution(4988515296718349389)
XLA Ops:
  0.6 2.8 broadcast_in_dim.15
  3.4 4.5 all-to-all-start
  8.6 27.9 %all-to-all-done = f32[4,1,192,768]{3,2,1,0:T(8,128)} async-done(((f32[4,1,192,768]{3,2,1,0:T(8,128)}), f32[4,1,192,768]{3,2,1,0:T(8,128)}, u32[]{:S(2)}, u32[]{:S(2)}) %all-to-all-start) | async-done | bytes 2359328 | tf_op jit(solution)/shard_map/all_to_all | solution.py:17
  36.6 9.1 %multiply_bitcast_fusion = (f32[1,768,768]{2,1,0:T(8,128)S(1)}, f32[1,1,768,768]{3,2,1,0:T(8,128)}) fusion(f32[]{:T(128)S(6)} %convert_element_type.4, f32[768,768]{1,0:T(8,128)} %bitcast.3, f32[1,1,768,768]{3,2,1,0:T(8,128)S(1)} %copy-done), kind=kOutput, calls=%fused_computation.17 | convolution fusion | flops 5436407808 | bytes 9437188 | tf_op jit(solution)/shard_map/dot_general | solution.py:33
  45.7 1.5 copy-done.2
  47.1 0.5 collective-permute-start
  47.6 51.9 %collective-permute-done = f32[1,768,768]{2,1,0:T(8,128)S(1)} collective-permute-done((f32[1,768,768]{2,1,0:T(8,128)S(1)}, f32[1,768,768]{2,1,0:T(8,128)S(1)}, u32[]{:S(2)}, u32[]{:S(2)}) %collective-permute-start) | collective-permute-done | bytes 2359328 | tf_op jit(solution)/shard_map/ppermute | solution.py:36
  99.5 51.6 %collective-permute-done.1 = f32[1,768,768]{2,1,0:T(8,128)} collective-permute-done((f32[1,768,768]{2,1,0:T(8,128)S(1)}, f32[1,768,768]{2,1,0:T(8,128)}, u32[]{:S(2)}, u32[]{:S(2)}) %collective-permute-start.1) | collective-permute-done | bytes 2359328 | tf_op jit(solution)/shard_map/ppermute | solution.py:36
  151.1 0.5 collective-permute-start.2
  151.7 50.8 %collective-permute-done.2 = f32[1,768,768]{2,1,0:T(8,128)} collective-permute-done((f32[1,768,768]{2,1,0:T(8,128)}, f32[1,768,768]{2,1,0:T(8,128)}, u32[]{:S(2)}, u32[]{:S(2)}) %collective-permute-start.2) | collective-permute-done | bytes 2359328 | tf_op jit(solution)/shard_map/ppermute | solution.py:36
  202.4 3.3 constant_dynamic-update-slice_fusion.7
  205.7 3.3 constant_dynamic-update-slice_fusion.6
  209.0 3.4 constant_dynamic-update-slice_fusion.5
  212.4 1.6 constant_dynamic-update-slice_fusion.4
  214.0 3.2 constant_dynamic-update-slice_fusion.3
  217.2 3.4 constant_dynamic-update-slice_fusion.2
  220.7 1.5 constant_dynamic-update-slice_fusion.1
  222.2 1.6 constant_dynamic-update-slice_fusion
  223.8 7.9 %constant_dynamic-slice_fusion = f32[4,768,768]{2,1,0:T(8,128)} fusion(f32[8,768,768]{2,1,0:T(8,128)} %constant_dynamic-update-slice_fusion, s32[]{:T(128)S(6)} %select_n.34), kind=kLoop, calls=%fused_computation.36 | loop fusion | bytes 18874372 | tf_op jit(solution)/shard_map/jit(_roll_dynamic)/dynamic_slice | solution.py:37
  231.6 11.8 %gather_fusion.1 = f32[7,768,768]{2,1,0:T(8,128)} fusion(f32[4,768,768]{2,1,0:T(8,128)} %constant_dynamic-slice_fusion, s32[1024]{0:T(1024)S(1)} %get-tuple-element.9), kind=kCustom, calls=%fused_computation.1 | custom fusion | bytes 33030172 | tf_op jit(solution)/shard_map/gather | solution.py:41
  243.4 11.8 %gather_fusion = f32[7,768,768]{2,1,0:T(8,128)} fusion(f32[4,768,768]{2,1,0:T(8,128)} %constant_dynamic-slice_fusion, s32[1024]{0:T(1024)S(1)} %get-tuple-element.10), kind=kCustom, calls=%fused_computation | custom fusion | bytes 33030172 | tf_op jit(solution)/shard_map/gather | solution.py:40
  255.2 44.7 %fusion.18 = f32[7,768,768]{2,1,0:T(8,128)} fusion(f32[7,768,768]{2,1,0:T(8,128)} %gather_fusion, f32[7,768,768]{2,1,0:T(8,128)} %gather_fusion.1), kind=kOutput, calls=%fused_computation.38 | convolution fusion | flops 38050725888 | bytes 49545216 | tf_op jit(solution)/shard_map/pij,pkj->pik/dot_general | solution.py:42
  300.0 27.3 %fusion = f32[5,768,768]{2,0,1:T(8,128)} fusion(f32[7,768,768]{2,1,0:T(8,128)} %fusion.18, s32[7]{0:T(128)S(1)} %bitcast.63), kind=kOutput, calls=%fused_computation.2 | convolution fusion | flops 247726112 | bytes 28311580 | tf_op jit(solution)/shard_map/dp,pik->dik/dot_general | solution.py:45
  327.2 39.2 %fusion.15 = (f32[1,768,768]{2,0,1:T(1,128)}, f32[1,768,768]{2,0,1:T(1,128)S(1)}, f32[1,768,768]{2,0,1:T(1,128)S(1)}, f32[1,768,768]{2,0,1:T(1,128)S(1)}, f32[1,768,768]{2,0,1:T(1,128)S(1)}) fusion(f32[5,768,768]{2,0,1:T(8,128)} %fusion), kind=kLoop, calls=%fused_computation.37 | loop fusion | bytes 23592960 | tf_op jit(solution)/shard_map/slice | solution.py:46
  367.1 6.7 %collective-permute-start.5 = (f32[768,768]{1,0:T(8,128)S(1)}, f32[768,768]{1,0:T(8,128)S(1)}, u32[]{:S(2)}, u32[]{:S(2)}) collective-permute-start(f32[768,768]{1,0:T(8,128)S(1)} %bitcast.61), channel_id=1, source_target_pairs={{0,12},{4,16},{8,20},{12,24},{16,28},{20,32},{24,36},{28,40},{32,4... | collective-permute-start | bytes 7077896 | tf_op jit(solution)/shard_map/ppermute | solution.py:26
  373.8 1.6 collective-permute-start.6
  375.4 1.2 collective-permute-start.4
  376.6 52.8 %collective-permute-done.5 = f32[768,768]{1,0:T(8,128)S(1)} collective-permute-done((f32[768,768]{1,0:T(8,128)S(1)}, f32[768,768]{1,0:T(8,128)S(1)}, u32[]{:S(2)}, u32[]{:S(2)}) %collective-permute-start.5) | collective-permute-done | bytes 2359328 | tf_op jit(solution)/shard_map/ppermute | solution.py:26
  429.4 46.2 %collective-permute-done.6 = f32[768,768]{1,0:T(8,128)S(1)} collective-permute-done((f32[768,768]{1,0:T(8,128)S(1)}, f32[768,768]{1,0:T(8,128)S(1)}, u32[]{:S(2)}, u32[]{:S(2)}) %collective-permute-start.6) | collective-permute-done | bytes 2359328 | tf_op jit(solution)/shard_map/ppermute | solution.py:26
  475.6 48.3 %collective-permute-done.3 = f32[768,768]{1,0:T(8,128)S(1)} collective-permute-done((f32[768,768]{1,0:T(8,128)S(1)}, f32[768,768]{1,0:T(8,128)S(1)}, u32[]{:S(2)}, u32[]{:S(2)}) %collective-permute-start.3) | collective-permute-done | bytes 2359328 | tf_op jit(solution)/shard_map/ppermute | solution.py:26
  523.9 32.6 %collective-permute-done.4 = f32[768,768]{1,0:T(8,128)S(1)} collective-permute-done((f32[768,768]{1,0:T(8,128)S(1)}, f32[768,768]{1,0:T(8,128)S(1)}, u32[]{:S(2)}, u32[]{:S(2)}) %collective-permute-start.4) | collective-permute-done | bytes 2359328 | tf_op jit(solution)/shard_map/ppermute | solution.py:26
  556.5 2.3 fusion.7
  (30 shorter events, 0.7 us)
Async XLA Ops:
  0.6 35.9 %copy-start = (f32[1,1,768,768]{3,2,1,0:T(8,128)S(1)}, f32[1,1,768,768]{3,2,1,0:T(8,128)}, u32[]{:S(2)}) copy-start(f32[1,1,768,768]{3,2,1,0:T(8,128)} %param.7) | copy-start | bytes 7077892
  3.4 33.1 %all-to-all-start = ((f32[4,1,192,768]{3,2,1,0:T(8,128)}), f32[4,1,192,768]{3,2,1,0:T(8,128)}, u32[]{:S(2)}, u32[]{:S(2)}) async-start(f32[4,1,192,768]{3,2,1,0:T(8,128)} %broadcast_in_dim.15), calls=%async_computation | async-start | bytes 4718592 | tf_op jit(solution)/shard_map/all_to_all | solution.py:17
  36.6 115.0 %copy-start.9 = (s32[1,1,7]{2,1,0:T(1,128)S(1)}, s32[1,1,7]{2,1,0:T(1,128)}, u32[]{:S(2)}) copy-start(s32[1,1,7]{2,1,0:T(1,128)} %param.11) | copy-start | bytes 88
  36.6 115.1 %copy-start.10 = (s32[1,1,7]{2,1,0:T(1,128)S(1)}, s32[1,1,7]{2,1,0:T(1,128)}, u32[]{:S(2)}) copy-start(s32[1,1,7]{2,1,0:T(1,128)} %param.12) | copy-start | bytes 88
  45.7 1.5 copy-start.2
  47.1 52.4 %collective-permute-start = (f32[1,768,768]{2,1,0:T(8,128)S(1)}, f32[1,768,768]{2,1,0:T(8,128)S(1)}, u32[]{:S(2)}, u32[]{:S(2)}) collective-permute-start(f32[1,768,768]{2,1,0:T(8,128)S(1)} %get-tuple-element.7), channel_id=1, source_target_pairs={{0,1},{1,2},{2,3},{3,0},{4,5},{5,6},{6,7},{7,4},{8,9},{9,10},{10,1... | collective-permute-start | bytes 7077896 | tf_op jit(solution)/shard_map/ppermute | solution.py:36
  99.5 106.2 %copy-start.5 = (f32[1,768,768]{2,1,0:T(8,128)}, f32[1,768,768]{2,1,0:T(8,128)S(1)}, u32[]{:S(2)}) copy-start(f32[1,768,768]{2,1,0:T(8,128)S(1)} %collective-permute-done) | copy-start | bytes 7077892
  99.5 51.6 %collective-permute-start.1 = (f32[1,768,768]{2,1,0:T(8,128)S(1)}, f32[1,768,768]{2,1,0:T(8,128)}, u32[]{:S(2)}, u32[]{:S(2)}) collective-permute-start(f32[1,768,768]{2,1,0:T(8,128)S(1)} %collective-permute-done), channel_id=1, source_target_pairs={{0,1},{1,2},{2,3},{3,0},{4,5},{5,6},{6,7},{7,4},{8,9},{9,10},{10,1... | collective-permute-start | bytes 7077896 | tf_op jit(solution)/shard_map/ppermute | solution.py:36
  151.1 51.3 %collective-permute-start.2 = (f32[1,768,768]{2,1,0:T(8,128)}, f32[1,768,768]{2,1,0:T(8,128)}, u32[]{:S(2)}, u32[]{:S(2)}) collective-permute-start(f32[1,768,768]{2,1,0:T(8,128)} %collective-permute-done.1), channel_id=1, source_target_pairs={{0,1},{1,2},{2,3},{3,0},{4,5},{5,6},{6,7},{7,4},{8,9},{9,10},{10,1... | collective-permute-start | bytes 7077896 | tf_op jit(solution)/shard_map/ppermute | solution.py:36
  209.0 3.4 copy-start.3
  217.2 3.4 copy-start.6
  255.2 44.8 %copy-start.8 = (s32[1,1,7]{2,1,0:T(1,128)S(1)}, s32[1,1,7]{2,1,0:T(1,128)}, u32[]{:S(2)}) copy-start(s32[1,1,7]{2,1,0:T(1,128)} %param.13) | copy-start | bytes 88
  366.9 189.6 %copy-start.4 = (f32[1,768,768]{2,0,1:T(1,128)S(1)}, f32[1,768,768]{2,0,1:T(1,128)}, u32[]{:S(2)}) copy-start(f32[1,768,768]{2,0,1:T(1,128)} %get-tuple-element.2) | copy-start | bytes 7077892
  366.9 189.6 %copy-start.7 = (f32[1,1,768,768]{3,2,1,0:T(8,128)S(1)}, f32[1,1,768,768]{3,2,1,0:T(8,128)}, u32[]{:S(2)}) copy-start(f32[1,1,768,768]{3,2,1,0:T(8,128)} %param.9) | copy-start | bytes 7077892
  367.1 62.3 %collective-permute-start.5 = (f32[768,768]{1,0:T(8,128)S(1)}, f32[768,768]{1,0:T(8,128)S(1)}, u32[]{:S(2)}, u32[]{:S(2)}) collective-permute-start(f32[768,768]{1,0:T(8,128)S(1)} %bitcast.61), channel_id=1, source_target_pairs={{0,12},{4,16},{8,20},{12,24},{16,28},{20,32},{24,36},{28,40},{32,4... | collective-permute-start | bytes 7077896 | tf_op jit(solution)/shard_map/ppermute | solution.py:26
  373.8 101.8 %collective-permute-start.6 = (f32[768,768]{1,0:T(8,128)S(1)}, f32[768,768]{1,0:T(8,128)S(1)}, u32[]{:S(2)}, u32[]{:S(2)}) collective-permute-start(f32[768,768]{1,0:T(8,128)S(1)} %bitcast.60), channel_id=1, source_target_pairs={{0,16},{4,20},{8,24},{12,28},{16,32},{20,36},{24,40},{28,44},{32,4... | collective-permute-start | bytes 7077896 | tf_op jit(solution)/shard_map/ppermute | solution.py:26
  375.4 148.5 %collective-permute-start.3 = (f32[768,768]{1,0:T(8,128)S(1)}, f32[768,768]{1,0:T(8,128)S(1)}, u32[]{:S(2)}, u32[]{:S(2)}) collective-permute-start(f32[768,768]{1,0:T(8,128)S(1)} %bitcast.59), channel_id=1, source_target_pairs={{0,4},{4,8},{8,12},{12,16},{16,20},{20,24},{24,28},{28,32},{32,36}... | collective-permute-start | bytes 7077896 | tf_op jit(solution)/shard_map/ppermute | solution.py:26
  375.4 181.1 %collective-permute-start.4 = (f32[768,768]{1,0:T(8,128)S(1)}, f32[768,768]{1,0:T(8,128)S(1)}, u32[]{:S(2)}, u32[]{:S(2)}) collective-permute-start(f32[768,768]{1,0:T(8,128)S(1)} %bitcast.58), channel_id=1, source_target_pairs={{0,8},{4,12},{8,16},{12,20},{16,24},{20,28},{24,32},{28,36},{32,40... | collective-permute-start | bytes 7077896 | tf_op jit(solution)/shard_map/ppermute | solution.py:26
  556.5 2.3 copy-start.1
